TPU v7x, 256 devices: a whole 4x4x8 slice. The times are simulated.
256 devices in a mesh: rep: 2 (over core), exp: 128 (over x, y, z).
Axes of the slice: x: 4, y: 4, z: 8, core: 2. Of those that a mesh axis runs over, the one named last changes fastest.
Arguments:
- attn_out: bfloat16 [16384, 4096], P(('rep', 'exp')), may hold values from -6 to 6
- out_weight: bfloat16 [4096, 2048], P('exp'), may hold values from -0.09375 to 0.09375
- router_weight: bfloat16 [2048, 128], replicated, may hold values from -0.125 to 0.125
- gate_weight: bfloat16 [128, 2048, 768], P('exp'), may hold values from -0.125 to 0.125
- up_weight: bfloat16 [128, 2048, 768], P('exp'), may hold values from -0.125 to 0.125
- down_weight: bfloat16 [128, 768, 2048], P('exp'), may hold values from -0.21875 to 0.21875
- cotangent: bfloat16 [16384, 2048], P(('rep', 'exp')), may hold values from -6 to 6
- log_ratios: float32 [16384], P(('rep', 'exp')), may hold values from -0.03 to 0.05
- expert_ids: int32 [16384, 8], P(('rep', 'exp')), may hold values from 0 to 127, as said below
- slot_ids: int32 [16384, 8], P(('rep', 'exp')), may hold values from 0 to 5, as said below
- episode_ids: int32 [16384], P(('rep', 'exp')), may hold values from 0 to 255, never falling along the last dimension, each value on 1 to 256 neighbouring positions
Outputs:
- token_grads: bfloat16 [16384, 4096], P(('rep', 'exp'))
- router_grad: float32 [2048, 128], P('exp')
Inputs may be any that keep to these rules, and one draw needn't show every extreme that they name: `expert_ids`: each row names 8 different experts. Among the rows of one device no expert is named more than 6 times, and on every device some expert is named exactly 6 times. `slot_ids`: among the rows of one device, the pairs of a row with one expert named in it get distinct slots; the slots of one expert on one device are 0 up to the number of its pairs there minus 1. `episode_ids`: episodes are runs of consecutive tokens, numbered in order; each has 1 to 256 tokens, one exactly 256.
All inputs are finite; a program needn't handle non-finite values.
Results may differ from a plain program's by a relative error of at most 0.012.
Values may be sent and summed in bfloat16 or wider, within the bound.
No kernel may reach another device: no remote copies, remote signals or barrier semaphores. Data moves between devices by JAX's collectives and lax.ppermute only.
A program may use at most 128 MiB of HBM per device.

v0:
```python
import jax
import jax.numpy as jnp
from jax import lax
from jax.sharding import PartitionSpec as P

clip_top = 4.0


def shards(
    attn_out,
    out_weight,
    router_weight,
    gate_weight,
    up_weight,
    down_weight,
    cotangent,
    log_ratios,
    expert_ids,
    slot_ids,
    episode_ids,
):
    tok_count = attn_out.shape[0]
    top_count = expert_ids.shape[1]
    model_width = cotangent.shape[1]
    expert_count = lax.axis_size("exp")
    device_count = lax.axis_size("rep") * expert_count
    capacity = 3 * tok_count * top_count // (2 * expert_count)
    episode_count = tok_count * device_count // 64
    episode_hits = (
        episode_ids[:, None] == jnp.arange(episode_count, dtype=jnp.int32)[None, :]
    ).astype(jnp.float32)
    part_logs = jnp.sum(episode_hits * log_ratios[:, None], axis=0)
    part_counts = jnp.sum(episode_hits, axis=0)
    log_sums, counts = lax.psum((part_logs, part_counts), ("rep", "exp"))
    episode_weight = jnp.minimum(jnp.exp(log_sums), clip_top)
    mean_weight = jnp.sum(counts * episode_weight) / (tok_count * device_count)
    token_scale = jnp.sum(episode_hits * episode_weight[None, :], axis=1) / mean_weight
    weight_full = lax.all_gather(out_weight, "exp", axis=0, tiled=True)
    hidden = jnp.dot(attn_out, weight_full, preferred_element_type=jnp.float32).astype(jnp.bfloat16)
    logits = jnp.dot(hidden, router_weight, preferred_element_type=jnp.float32)
    expert_hits = (expert_ids[:, :, None] == jnp.arange(expert_count, dtype=jnp.int32)).astype(
        jnp.float32
    )
    chosen = jnp.sum(expert_hits * logits[:, None, :], axis=2)
    raised = jnp.exp(chosen)
    gate_probs = raised / jnp.sum(raised, axis=1, keepdims=True)
    targets = expert_ids * capacity + slot_ids
    slot_count = expert_count * capacity
    labels = jnp.arange(tok_count, dtype=jnp.int32)[:, None] + 1
    matches = (targets[:, :, None] == jnp.arange(slot_count, dtype=jnp.int32)).astype(jnp.int32)
    owners = jnp.sum(matches * labels[:, :, None], axis=(0, 1))
    filled = owners > 0
    source_rows = jnp.maximum(owners - 1, 0)
    zero_value = jnp.zeros((), jnp.bfloat16)
    send_hidden = jnp.where(filled[:, None], hidden[source_rows], zero_value).reshape(
        expert_count, capacity, model_width
    )
    send_cot = jnp.where(filled[:, None], cotangent[source_rows], zero_value).reshape(
        expert_count, capacity, model_width
    )
    rows_in = lax.all_to_all(send_hidden, "exp", split_axis=0, concat_axis=0, tiled=True)
    cot_in = lax.all_to_all(send_cot, "exp", split_axis=0, concat_axis=0, tiled=True)
    gate_pre = jnp.einsum(
        "snd,df->snf", rows_in, gate_weight[0], preferred_element_type=jnp.float32
    )
    up_pre = jnp.einsum("snd,df->snf", rows_in, up_weight[0], preferred_element_type=jnp.float32)
    upstream = jnp.einsum("snd,fd->snf", cot_in, down_weight[0], preferred_element_type=jnp.float32)
    sigmoid_gate = jax.nn.sigmoid(gate_pre)
    slot_score = jnp.sum(upstream * (gate_pre * sigmoid_gate * up_pre), axis=2)
    grad_gate = (upstream * up_pre * sigmoid_gate * (1.0 + gate_pre * (1.0 - sigmoid_gate))).astype(
        jnp.bfloat16
    )
    grad_up = (upstream * gate_pre * sigmoid_gate).astype(jnp.bfloat16)
    back_rows = (
        jnp.einsum("snf,df->snd", grad_gate, gate_weight[0], preferred_element_type=jnp.float32)
        + jnp.einsum("snf,df->snd", grad_up, up_weight[0], preferred_element_type=jnp.float32)
    ).astype(jnp.bfloat16)
    back_home = lax.all_to_all(back_rows, "exp", split_axis=0, concat_axis=0, tiled=True)
    score_home = lax.all_to_all(slot_score, "exp", split_axis=0, concat_axis=0, tiled=True)
    pair_back = back_home.reshape(slot_count, model_width)[targets]
    pair_score = score_home.reshape(slot_count)[targets]
    mixed_back = jnp.sum(gate_probs[:, :, None] * pair_back.astype(jnp.float32), axis=1)
    logit_grad = gate_probs * (pair_score - jnp.sum(gate_probs * pair_score, axis=1, keepdims=True))
    full_grad = jnp.sum(expert_hits * logit_grad[:, :, None], axis=1)
    weighted = (token_scale[:, None] * full_grad).astype(jnp.bfloat16)
    router_part = jnp.einsum("td,te->de", hidden, weighted, preferred_element_type=jnp.float32)
    grad_hidden = (
        token_scale[:, None] * mixed_back
        + jnp.dot(weighted, router_weight.T, preferred_element_type=jnp.float32)
    ).astype(jnp.bfloat16)
    token_grads = jnp.dot(grad_hidden, weight_full.T, preferred_element_type=jnp.float32).astype(
        jnp.bfloat16
    )
    router_total = lax.psum(router_part, ("rep", "exp"))
    row_count = model_width // expert_count
    router_grad = lax.dynamic_slice_in_dim(
        router_total, lax.axis_index("exp") * row_count, row_count, 0
    )
    return (token_grads, router_grad)


def solution(mesh):
    placed = (
        P(("rep", "exp"), None),
        P("exp", None),
        P(),
        P("exp", None, None),
        P("exp", None, None),
        P("exp", None, None),
        P(("rep", "exp"), None),
        P(("rep", "exp")),
        P(("rep", "exp"), None),
        P(("rep", "exp"), None),
        P(("rep", "exp")),
    )
    return jax.shard_map(
        shards,
        mesh=mesh,
        in_specs=placed,
        out_specs=(P(("rep", "exp"), None), P("exp", None)),
        check_vma=False,
    )
```

profile of v0, /device:TPU:2, one launch (start us, length us, event | category | flops | bytes accessed | tf_op | source)
XLA Modules:
  0.0 948.8 jit_solution(6600559267684554942)
XLA Ops:
  7.2 0.0 copy-start
  7.2 0.0 all-gather.2.cloned.1.call-start
  7.2 0.7 all-gather.2.cloned.1.call-update
  7.9 0.8 compare_select_fusion
  8.7 0.1 copy.31
  8.8 0.2 select_reduce_fusion
  9.1 0.2 gt.11
  9.3 4.3 gather_fusion
  13.5 6.3 gather.17
  19.8 144.6 %all-gather.2.cloned.1.call-done = bf16[4096,2048]{1,0:T(8,128)(2,1)} async-done(((bf16[32,2048]{1,0:T(8,128)(2,1)}), bf16[4096,2048]{1,0:T(8,128)(2,1)}) %all-gather.2.cloned.1.call-update) | async-done | bytes 16777232 | tf_op jit(solution)/shard_map/all_gather | solution.py:38
  164.4 9.0 convolution_convert_fusion.1
  173.4 4.3 gather_fusion.1
  177.7 6.2 gather.19
  184.0 5.2 broadcast_select_fusion.1
  189.2 106.0 %all_to_all.24 = bf16[128,6,2048]{2,1,0:T(8,128)(2,1)} all-to-all(bf16[128,6,2048]{2,1,0:T(8,128)(2,1)S(1)} %get-tuple-element.9), channel_id=1, replica_groups=mesh['rep'=2,'exp'=128] {'exp'}, dimensions={0} | all-to-all | bytes 6291456 | tf_op jit(solution)/shard_map/all_to_all | solution.py:61
  295.2 10.3 %all-to-all-start = ((bf16[128,6,2048]{2,1,0:T(8,128)(2,1)}), bf16[128,6,2048]{2,1,0:T(8,128)(2,1)}, u32[]{:S(2)}, u32[]{:S(2)}) async-start(bf16[128,6,2048]{2,1,0:T(8,128)(2,1)} %get-tuple-element.8), calls=%async_computation | async-start | bytes 8388608 | tf_op jit(solution)/shard_map/all_to_all | solution.py:62
  305.5 0.0 copy-done
  305.5 0.0 copy-start.3
  305.5 0.0 copy-start.8
  305.6 9.3 fusion.3
  314.9 7.5 fusion.6
  322.4 76.0 %all-to-all-done = bf16[128,6,2048]{2,1,0:T(8,128)(2,1)} async-done(((bf16[128,6,2048]{2,1,0:T(8,128)(2,1)}), bf16[128,6,2048]{2,1,0:T(8,128)(2,1)}, u32[]{:S(2)}, u32[]{:S(2)}) %all-to-all-start) | async-done | bytes 3145760 | tf_op jit(solution)/shard_map/all_to_all | solution.py:62
  398.5 11.8 %multiply_reduce_fusion = (f32[128,6]{0,1:T(8,128)S(1)}, f32[128,6,768]{2,0,1:T(8,128)}) fusion(f32[128,6,768]{2,0,1:T(8,128)} %fusion.6, f32[128,6,768]{2,0,1:T(8,128)} %fusion.3, bf16[1,768,2048]{2,1,0:T(8,128)(2,1)} %param.16, bf16[128,6,2048]{2,1,0:T(8,128)(2,1)} %all-to-all-done), kind=kOutput, calls=%fused_computation.20 | convolution fusion | flops 2420047104 | bytes 13372416 | tf_op jit(solution)/shard_map/snd,fd->snf/dot_general | solution.py:67
  410.3 0.7 copy.37
  411.1 8.7 all-to-all-start.3
  419.8 0.0 copy-start.9
  419.8 0.0 copy-start.10
  419.8 0.0 copy-start.11
  419.8 5.6 fusion.1
  425.4 0.0 copy-done.9
  425.4 0.0 copy-done.10
  425.4 2.9 add_convert_fusion
  428.3 3.7 copy.35
  432.1 0.0 all-to-all-done.3
  432.1 14.4 %all-to-all-start.2 = ((bf16[128,6,2048]{2,1,0:T(8,128)(2,1)}), bf16[128,6,2048]{2,1,0:T(8,128)(2,1)}, u32[]{:S(2)}, u32[]{:S(2)}) async-start(bf16[128,6,2048]{2,1,0:T(8,128)(2,1)} %copy.35), calls=%async_computation.2 | async-start | bytes 8388608 | tf_op jit(solution)/shard_map/all_to_all | solution.py:78
  446.5 0.0 all-reduce.2.cloned.1.call-start
  446.5 0.1 copy.30
  446.6 0.1 copy.36
  446.7 0.1 reshape.135
  446.8 0.1 select_reduce_fusion.4
  446.9 130.2 %psum.21 = f32[256]{0:T(256)S(1)} all-reduce(f32[256]{0:T(256)S(1)} %select_reduce_fusion.4), channel_id=1, replica_groups=mesh['rep'=2,'exp'=128] {'rep','exp'}, use_global_device_ids=true, to_apply=%region_1.0 | all-reduce | flops 256 | bytes 2048 | tf_op jit(solution)/shard_map/psum | solution.py:34
  577.1 0.2 convert_reduce_fusion
  577.3 74.9 %psum.22 = f32[256]{0:T(256)S(1)} all-reduce(f32[256]{0:T(256)S(1)} %get-tuple-element.2), channel_id=1, replica_groups=mesh['rep'=2,'exp'=128] {'rep','exp'}, use_global_device_ids=true, to_apply=%region_4.0 | all-reduce | flops 256 | bytes 2048 | tf_op jit(solution)/shard_map/psum | solution.py:34
  652.2 0.6 multiply_reduce_fusion.2
  653.5 0.2 fusion.21
  653.7 0.2 select_reduce_fusion.2
  653.9 0.1 exponential_reduce_fusion
  654.1 0.5 broadcast.151
  654.6 0.8 reduce.3
  655.4 0.1 reshape.116
  655.5 2.3 gather_fusion.3
  657.8 0.1 reshape.142
  657.9 0.2 multiply_reduce_fusion.1
  658.1 0.1 subtract_multiply_fusion
  658.2 0.2 select_reduce_fusion.1
  658.4 1.3 fusion.20
  659.7 0.0 all-reduce.2.cloned.1.call-update
  659.8 255.7 %all-reduce.2.cloned.1.call-done = f32[2048,128]{1,0:T(8,128)} async-done(((f32[2048,128]{1,0:T(8,128)}), f32[2048,128]{1,0:T(8,128)}) %all-reduce.2.cloned.1.call-update) | async-done | bytes 1048592 | tf_op jit(solution)/shard_map/psum | solution.py:94
  915.5 1.3 constant_dynamic-slice_fusion
  916.8 0.0 all-to-all-done.2
  916.8 4.9 reshape.115
  921.7 3.3 gather_fusion.2
  925.0 4.2 fusion
  929.2 12.5 %convolution_convert_fusion = bf16[64,4096]{1,0:T(8,128)(2,1)} fusion(bf16[4096,2048]{1,0:T(8,128)(2,1)} %all-gather.2.cloned.1.call-done, bf16[2048,128]{1,0:T(8,128)(2,1)} %param.13, f32[64,2048]{1,0:T(8,128)} %fusion, f32[64]{0:T(128)S(1)} %broadcast_divide_fusion, f32[64,128]{1,0:T(8,128)S(1)} %select_reduce_fusion.1), kind=kOutput, calls=%fused_computation.5 | convolution fusion | flops 1107968000 | bytes 18383104 | tf_op jit(solution)/shard_map/dot_general | solution.py:91
  (22 shorter events, 0.1 us)
Async XLA Ops:
  7.2 298.4 %copy-start = (bf16[1,2048,768]{2,1,0:T(8,128)(2,1)S(1)}, bf16[1,2048,768]{2,1,0:T(8,128)(2,1)}, u32[]{:S(2)}) copy-start(bf16[1,2048,768]{2,1,0:T(8,128)(2,1)} %param.14) | copy-start | bytes 9437188
  7.2 2.1 copy-start.2
  7.2 157.2 %all-gather.2.cloned.1.call-start = ((), (), s32[]{:S(2)}) async-start(), calls=%async_computation.4 | async-start | bytes 16908288 | tf_op jit(solution)/shard_map/all_gather | solution.py:38
  295.2 103.3 %all-to-all-start = ((bf16[128,6,2048]{2,1,0:T(8,128)(2,1)}), bf16[128,6,2048]{2,1,0:T(8,128)(2,1)}, u32[]{:S(2)}, u32[]{:S(2)}) async-start(bf16[128,6,2048]{2,1,0:T(8,128)(2,1)} %get-tuple-element.8), calls=%async_computation | async-start | bytes 8388608 | tf_op jit(solution)/shard_map/all_to_all | solution.py:62
  305.5 9.4 copy-start.3
  305.5 9.4 copy-start.8
  411.1 21.0 %all-to-all-start.3 = ((f32[128,1,6]{2,1,0:T(1,128)}), f32[128,1,6]{2,1,0:T(1,128)S(1)}, u32[]{:S(2)}, u32[]{:S(2)}) async-start(f32[128,1,6]{2,1,0:T(1,128)} %copy.37), calls=%async_computation.3 | async-start | bytes 131072 | tf_op jit(solution)/shard_map/all_to_all | solution.py:79
  419.8 5.6 copy-start.9
  419.8 5.6 copy-start.10
  419.8 5.6 copy-start.11
  432.0 14.5 %copy-start.5 = (s32[64,8]{0,1:T(8,128)S(1)}, s32[64,8]{0,1:T(8,128)}, u32[]{:S(2)}) copy-start(s32[64,8]{0,1:T(8,128)} %param.19) | copy-start | bytes 6148
  432.0 14.8 %copy-start.6 = (s32[64]{0:T(128)S(1)}, s32[64]{0:T(128)}, u32[]{:S(2)}) copy-start(s32[64]{0:T(128)} %param.21) | copy-start | bytes 772
  432.0 14.8 %copy-start.7 = (f32[64]{0:T(128)S(1)}, f32[64]{0:T(128)}, u32[]{:S(2)}) copy-start(f32[64]{0:T(128)} %param.18) | copy-start | bytes 772
  432.1 221.4 %copy-start.4 = (bf16[2048,128]{1,0:T(8,128)(2,1)S(1)}, bf16[2048,128]{1,0:T(8,128)(2,1)}, u32[]{:S(2)}) copy-start(bf16[2048,128]{1,0:T(8,128)(2,1)} %param.13) | copy-start | bytes 1572868
  432.1 484.7 %all-to-all-start.2 = ((bf16[128,6,2048]{2,1,0:T(8,128)(2,1)}), bf16[128,6,2048]{2,1,0:T(8,128)(2,1)}, u32[]{:S(2)}, u32[]{:S(2)}) async-start(bf16[128,6,2048]{2,1,0:T(8,128)(2,1)} %copy.35), calls=%async_computation.2 | async-start | bytes 8388608 | tf_op jit(solution)/shard_map/all_to_all | solution.py:78
  446.5 469.0 %all-reduce.2.cloned.1.call-start = ((), (), s32[]{:S(2)}) async-start(), calls=%async_computation.5 | async-start | bytes 2097152 | tf_op jit(solution)/shard_map/psum | solution.py:94
  929.2 12.5 %copy-start.1 = (bf16[1,2048,768]{2,1,0:T(8,128)(2,1)S(1)}, bf16[1,2048,768]{2,1,0:T(8,128)(2,1)}, u32[]{:S(2)}) copy-start(bf16[1,2048,768]{2,1,0:T(8,128)(2,1)} %param.14) | copy-start | bytes 9437188
Sparse Core Ops, SparseCore 0:
  11.6 152.7 all-gather.1
  659.9 255.5 all-reduce.1
where the time goes:
time: 957 us; the launch traced here: 949 us
  waiting for transfers between devices  477 us (50%)
  blocking collectives  311 us (32%)
  matrix products  60.2 us (6%)
  local copies, waits for them, and re-layouts  38.7 us (4%)
  starting transfers between devices  33.5 us (4%)
  between operations  15.2 us (2%)
  other arithmetic  13 us (1%)
    psum x1, waiting for transfers between devices, shards(): router_total = lax.psum(router_part, ('rep', 'exp'))  256 us
    psum x2, blocking collectives, shards(): log_sums, counts = lax.psum((part_logs, part_counts), ('rep', 'exp'))  205 us
    all_gather x1, waiting for transfers between devices, shards(): weight_full = lax.all_gather(out_weight, 'exp', axis=0, tiled=True)  145 us
    all_to_all x1, blocking collectives, shards(): lax.all_to_all(send_hidden, 'exp', split_axis=0, concat_axis=0, tiled=True)  106 us
    all_to_all x1, waiting for transfers between devices, shards(): lax.all_to_all(send_cot, 'exp', split_axis=0, concat_axis=0, tiled=True)  76 us
  transfers between devices with their start and end apart: 5, of which 3 were waited for; matrix products, arithmetic and copies ran while one was open for 5% of the time, Pallas kernels for 0%

commit v1 on v0

--- a/solution.py
+++ b/solution.py
@@ -91,7 +91,7 @@
     token_grads = jnp.dot(grad_hidden, weight_full.T, preferred_element_type=jnp.float32).astype(
         jnp.bfloat16
     )
-    router_total = lax.psum(router_part, ("rep", "exp"))
+    router_total = lax.psum(lax.psum(router_part, "exp"), "rep")
     row_count = model_width // expert_count
     router_grad = lax.dynamic_slice_in_dim(
         router_total, lax.axis_index("exp") * row_count, row_count, 0

time: 957 us -> 952 us (level)
    psum x1 -> x2, waiting for transfers between devices: 256 us -> 250 us  [shards(): router_total = lax.psum(lax.psum(router_part, 'exp'), 'rep')]
  transfers between devices with their start and end apart: 5 -> 6, of which waited for: 3 -> 4; matrix products, arithmetic and copies ran while one was open for 5% -> 5% of each run, Pallas kernels for 0% -> 0%
where the time goes in v1:
time: 952 us; the launch traced here: 943 us
  waiting for transfers between devices  472 us (50%)
  blocking collectives  311 us (33%)
  matrix products  60.2 us (6%)
  local copies, waits for them, and re-layouts  38.7 us (4%)
  starting transfers between devices  33.5 us (4%)
  between operations  14.9 us (2%)
  other arithmetic  13 us (1%)
    psum x2, waiting for transfers between devices, shards(): router_total = lax.psum(lax.psum(router_part, 'exp'), 'rep')  250 us
    psum x2, blocking collectives, shards(): log_sums, counts = lax.psum((part_logs, part_counts), ('rep', 'exp'))  205 us
    all_gather x1, waiting for transfers between devices, shards(): weight_full = lax.all_gather(out_weight, 'exp', axis=0, tiled=True)  145 us
    all_to_all x1, blocking collectives, shards(): lax.all_to_all(send_hidden, 'exp', split_axis=0, concat_axis=0, tiled=True)  106 us
    all_to_all x1, waiting for transfers between devices, shards(): lax.all_to_all(send_cot, 'exp', split_axis=0, concat_axis=0, tiled=True)  76 us
  transfers between devices with their start and end apart: 6, of which 4 were waited for; matrix products, arithmetic and copies ran while one was open for 5% of the time, Pallas kernels for 0%

profile of v1, /device:TPU:2, one launch (start us, length us, event | category | flops | bytes accessed | tf_op | source)
XLA Modules:
  0.0 943.1 jit_solution(17831124089875176316)
XLA Ops:
  7.2 0.0 copy-start
  7.2 0.0 all-gather.2.cloned.1.call-start
  7.2 0.7 all-gather.2.cloned.1.call-update
  7.9 0.8 compare_select_fusion
  8.7 0.1 copy.31
  8.8 0.2 select_reduce_fusion
  9.1 0.2 gt.11
  9.3 4.3 gather_fusion
  13.5 6.3 gather.17
  19.8 144.6 %all-gather.2.cloned.1.call-done = bf16[4096,2048]{1,0:T(8,128)(2,1)} async-done(((bf16[32,2048]{1,0:T(8,128)(2,1)}), bf16[4096,2048]{1,0:T(8,128)(2,1)}) %all-gather.2.cloned.1.call-update) | async-done | bytes 16777232 | tf_op jit(solution)/shard_map/all_gather | solution.py:38
  164.4 9.0 convolution_convert_fusion.1
  173.4 4.3 gather_fusion.1
  177.7 6.2 gather.19
  184.0 5.2 broadcast_select_fusion.1
  189.2 106.0 %all_to_all.24 = bf16[128,6,2048]{2,1,0:T(8,128)(2,1)} all-to-all(bf16[128,6,2048]{2,1,0:T(8,128)(2,1)S(1)} %get-tuple-element.9), channel_id=1, replica_groups=mesh['rep'=2,'exp'=128] {'exp'}, dimensions={0} | all-to-all | bytes 6291456 | tf_op jit(solution)/shard_map/all_to_all | solution.py:61
  295.2 10.3 %all-to-all-start = ((bf16[128,6,2048]{2,1,0:T(8,128)(2,1)}), bf16[128,6,2048]{2,1,0:T(8,128)(2,1)}, u32[]{:S(2)}, u32[]{:S(2)}) async-start(bf16[128,6,2048]{2,1,0:T(8,128)(2,1)} %get-tuple-element.8), calls=%async_computation | async-start | bytes 8388608 | tf_op jit(solution)/shard_map/all_to_all | solution.py:62
  305.5 0.0 copy-done
  305.5 0.0 copy-start.3
  305.5 0.0 copy-start.8
  305.6 9.3 fusion.3
  314.9 7.5 fusion.6
  322.4 76.0 %all-to-all-done = bf16[128,6,2048]{2,1,0:T(8,128)(2,1)} async-done(((bf16[128,6,2048]{2,1,0:T(8,128)(2,1)}), bf16[128,6,2048]{2,1,0:T(8,128)(2,1)}, u32[]{:S(2)}, u32[]{:S(2)}) %all-to-all-start) | async-done | bytes 3145760 | tf_op jit(solution)/shard_map/all_to_all | solution.py:62
  398.5 11.8 %multiply_reduce_fusion = (f32[128,6]{0,1:T(8,128)S(1)}, f32[128,6,768]{2,0,1:T(8,128)}) fusion(f32[128,6,768]{2,0,1:T(8,128)} %fusion.6, f32[128,6,768]{2,0,1:T(8,128)} %fusion.3, bf16[1,768,2048]{2,1,0:T(8,128)(2,1)} %param.16, bf16[128,6,2048]{2,1,0:T(8,128)(2,1)} %all-to-all-done), kind=kOutput, calls=%fused_computation.20 | convolution fusion | flops 2420047104 | bytes 13372416 | tf_op jit(solution)/shard_map/snd,fd->snf/dot_general | solution.py:67
  410.3 0.7 copy.37
  411.1 8.7 all-to-all-start.3
  419.8 0.0 copy-start.9
  419.8 0.0 copy-start.10
  419.8 5.6 fusion.1
  425.4 2.9 add_convert_fusion
  428.3 3.7 copy.35
  432.1 0.0 all-to-all-done.3
  432.1 14.4 %all-to-all-start.2 = ((bf16[128,6,2048]{2,1,0:T(8,128)(2,1)}), bf16[128,6,2048]{2,1,0:T(8,128)(2,1)}, u32[]{:S(2)}, u32[]{:S(2)}) async-start(bf16[128,6,2048]{2,1,0:T(8,128)(2,1)} %copy.35), calls=%async_computation.2 | async-start | bytes 8388608 | tf_op jit(solution)/shard_map/all_to_all | solution.py:78
  446.5 0.0 all-reduce.3.cloned.1.call-start
  446.5 0.1 copy.30
  446.6 0.1 copy.36
  446.7 0.1 reshape.135
  446.8 0.1 select_reduce_fusion.4
  446.9 130.2 %psum.28 = f32[256]{0:T(256)S(1)} all-reduce(f32[256]{0:T(256)S(1)} %select_reduce_fusion.4), channel_id=1, replica_groups=mesh['rep'=2,'exp'=128] {'rep','exp'}, use_global_device_ids=true, to_apply=%region_1.0 | all-reduce | flops 256 | bytes 2048 | tf_op jit(solution)/shard_map/psum | solution.py:34
  577.1 0.2 convert_reduce_fusion
  577.3 74.9 %psum.29 = f32[256]{0:T(256)S(1)} all-reduce(f32[256]{0:T(256)S(1)} %get-tuple-element.2), channel_id=1, replica_groups=mesh['rep'=2,'exp'=128] {'rep','exp'}, use_global_device_ids=true, to_apply=%region_4.0 | all-reduce | flops 256 | bytes 2048 | tf_op jit(solution)/shard_map/psum | solution.py:34
  652.2 0.6 multiply_reduce_fusion.2
  653.5 0.2 fusion.21
  653.7 0.2 select_reduce_fusion.2
  653.9 0.1 exponential_reduce_fusion
  654.0 0.5 broadcast.151
  654.6 0.8 reduce.3
  655.4 0.1 reshape.116
  655.5 2.3 gather_fusion.3
  657.8 0.1 reshape.142
  657.9 0.2 multiply_reduce_fusion.1
  658.1 0.1 subtract_multiply_fusion
  658.2 0.2 select_reduce_fusion.1
  658.4 1.3 fusion.20
  659.7 0.0 all-reduce.3.cloned.1.call-update
  659.8 0.0 all-reduce.5.cloned.1.call-start
  659.8 220.1 %all-reduce.3.cloned.1.call-done = f32[2048,128]{1,0:T(8,128)} async-done(((f32[2048,128]{1,0:T(8,128)}), f32[2048,128]{1,0:T(8,128)}) %all-reduce.3.cloned.1.call-update) | async-done | bytes 1048592 | tf_op jit(solution)/shard_map/psum | solution.py:94
  879.9 0.0 all-reduce.5.cloned.1.call-update
  879.9 30.2 %all-reduce.5.cloned.1.call-done = f32[2048,128]{1,0:T(8,128)} async-done(((f32[2048,128]{1,0:T(8,128)}), f32[2048,128]{1,0:T(8,128)}) %all-reduce.5.cloned.1.call-update) | async-done | bytes 1048592 | tf_op jit(solution)/shard_map/psum | solution.py:94
  910.1 1.3 constant_dynamic-slice_fusion
  911.4 0.0 all-to-all-done.2
  911.4 4.9 reshape.115
  916.3 3.3 gather_fusion.2
  919.6 4.2 fusion
  923.9 12.5 %convolution_convert_fusion = bf16[64,4096]{1,0:T(8,128)(2,1)} fusion(bf16[4096,2048]{1,0:T(8,128)(2,1)} %all-gather.2.cloned.1.call-done, bf16[2048,128]{1,0:T(8,128)(2,1)} %param.13, f32[64,2048]{1,0:T(8,128)} %fusion, f32[64]{0:T(128)S(1)} %broadcast_divide_fusion, f32[64,128]{1,0:T(8,128)S(1)} %select_reduce_fusion.1), kind=kOutput, calls=%fused_computation.5 | convolution fusion | flops 1107968000 | bytes 18383104 | tf_op jit(solution)/shard_map/dot_general | solution.py:91
  (25 shorter events, 0.1 us)
Async XLA Ops:
  7.2 298.4 %copy-start = (bf16[1,2048,768]{2,1,0:T(8,128)(2,1)S(1)}, bf16[1,2048,768]{2,1,0:T(8,128)(2,1)}, u32[]{:S(2)}) copy-start(bf16[1,2048,768]{2,1,0:T(8,128)(2,1)} %param.14) | copy-start | bytes 9437188
  7.2 2.1 copy-start.2
  7.2 157.2 %all-gather.2.cloned.1.call-start = ((), (), s32[]{:S(2)}) async-start(), calls=%async_computation.4 | async-start | bytes 16908288 | tf_op jit(solution)/shard_map/all_gather | solution.py:38
  295.2 103.3 %all-to-all-start = ((bf16[128,6,2048]{2,1,0:T(8,128)(2,1)}), bf16[128,6,2048]{2,1,0:T(8,128)(2,1)}, u32[]{:S(2)}, u32[]{:S(2)}) async-start(bf16[128,6,2048]{2,1,0:T(8,128)(2,1)} %get-tuple-element.8), calls=%async_computation | async-start | bytes 8388608 | tf_op jit(solution)/shard_map/all_to_all | solution.py:62
  305.5 9.4 copy-start.3
  305.5 9.4 copy-start.8
  411.1 21.0 %all-to-all-start.3 = ((f32[128,1,6]{2,1,0:T(1,128)}), f32[128,1,6]{2,1,0:T(1,128)S(1)}, u32[]{:S(2)}, u32[]{:S(2)}) async-start(f32[128,1,6]{2,1,0:T(1,128)} %copy.37), calls=%async_computation.3 | async-start | bytes 131072 | tf_op jit(solution)/shard_map/all_to_all | solution.py:79
  419.8 5.6 copy-start.9
  419.8 5.6 copy-start.10
  419.8 5.6 copy-start.11
  432.0 14.5 %copy-start.5 = (s32[64,8]{0,1:T(8,128)S(1)}, s32[64,8]{0,1:T(8,128)}, u32[]{:S(2)}) copy-start(s32[64,8]{0,1:T(8,128)} %param.19) | copy-start | bytes 6148
  432.0 14.8 %copy-start.6 = (s32[64]{0:T(128)S(1)}, s32[64]{0:T(128)}, u32[]{:S(2)}) copy-start(s32[64]{0:T(128)} %param.21) | copy-start | bytes 772
  432.0 14.8 %copy-start.7 = (f32[64]{0:T(128)S(1)}, f32[64]{0:T(128)}, u32[]{:S(2)}) copy-start(f32[64]{0:T(128)} %param.18) | copy-start | bytes 772
  432.1 221.4 %copy-start.4 = (bf16[2048,128]{1,0:T(8,128)(2,1)S(1)}, bf16[2048,128]{1,0:T(8,128)(2,1)}, u32[]{:S(2)}) copy-start(bf16[2048,128]{1,0:T(8,128)(2,1)} %param.13) | copy-start | bytes 1572868
  432.1 479.4 %all-to-all-start.2 = ((bf16[128,6,2048]{2,1,0:T(8,128)(2,1)}), bf16[128,6,2048]{2,1,0:T(8,128)(2,1)}, u32[]{:S(2)}, u32[]{:S(2)}) async-start(bf16[128,6,2048]{2,1,0:T(8,128)(2,1)} %copy.35), calls=%async_computation.2 | async-start | bytes 8388608 | tf_op jit(solution)/shard_map/all_to_all | solution.py:78
  446.5 433.4 %all-reduce.3.cloned.1.call-start = ((), (), s32[]{:S(2)}) async-start(), calls=%async_computation.5 | async-start | bytes 2097152 | tf_op jit(solution)/shard_map/psum | solution.py:94
  659.8 250.4 %all-reduce.5.cloned.1.call-start = ((), (), s32[]{:S(2)}) async-start(), calls=%async_computation.6 | async-start | bytes 2097152 | tf_op jit(solution)/shard_map/psum | solution.py:94
  923.9 12.5 %copy-start.1 = (bf16[1,2048,768]{2,1,0:T(8,128)(2,1)S(1)}, bf16[1,2048,768]{2,1,0:T(8,128)(2,1)}, u32[]{:S(2)}) copy-start(bf16[1,2048,768]{2,1,0:T(8,128)(2,1)} %param.14) | copy-start | bytes 9437188
Sparse Core Ops, SparseCore 0:
  11.6 152.7 all-gather.1
  659.9 219.9 all-reduce.2
  882.5 27.6 all-reduce.4
